TPU v7x, 32 devices: a whole 2x2x4 slice. The times are simulated.
32 devices in a mesh: item: 8 (over z, x), bucket: 4 (over y, core).
Axes of the slice: x: 2, y: 2, z: 4, core: 2. Of those that a mesh axis runs over, the one named last changes fastest.
Arguments:
- code_rows: bfloat16 [8192, 64], P('item'), may hold values from -6 to 6
- centroids: bfloat16 [32768, 64], P('bucket'), may hold values from -0.5 to 0.5
Outputs:
- grad_codes: float32 [8192, 64], P('item')
- new_centroids: float32 [32768, 64], P('bucket')
All inputs are finite; a program needn't handle non-finite values.
Results may differ from a plain program's by a relative error of at most 0.0032.
Values sent between devices are 32-bit elements; how exact they have to be, the bound alone decides.
No kernel may reach another device: no remote copies, remote signals or barrier semaphores. Data moves between devices by JAX's collectives and lax.ppermute only.
A program may use at most 128 MiB of HBM per device.

v0:
```python
import jax
import jax.numpy as jnp
from jax import lax
from jax.sharding import PartitionSpec as P

BUCKETS = 32768
ITERS = 3
score_scale = 20.0
step_rate = 0.2
epsilon = 1e-06


def joined(value, axis, join):
    pieces = jax.tree.map(lambda part: lax.all_gather(part, axis), value)
    head = jax.tree.map(lambda part: part[0], pieces)
    tail = jax.tree.map(lambda part: part[1:], pieces)
    so_far, _ = lax.scan(lambda so_far, piece: (join(so_far, piece), None), head, tail)
    return so_far


def scores_of(code_rows, centroids):
    return score_scale * lax.dot_general(
        code_rows, centroids, (((1,), (1,)), ((), ())), preferred_element_type=jnp.float32
    )


def lse_pair(first, second):
    highest = jnp.maximum(first[0], second[0])
    return (
        highest,
        first[1] * jnp.exp(first[0] - highest) + second[1] * jnp.exp(second[0] - highest),
    )


def stats_triple(first, second):
    highest = jnp.maximum(first[0], second[0])
    return (
        highest,
        first[1] * jnp.exp(first[0] - highest) + second[1] * jnp.exp(second[0] - highest),
        first[2] + second[2],
    )


def reduce_rows(values):
    highest = jnp.max(values, axis=1)
    summed = jnp.sum(jnp.exp(values - highest[:, None]), axis=1)
    highest, summed = joined((highest, summed), "bucket", lse_pair)
    return highest + jnp.log(summed)


def reduce_cols(values):
    highest = jnp.max(values, axis=0)
    summed = jnp.sum(jnp.exp(values - highest[None, :]), axis=0)
    highest, summed = joined((highest, summed), "item", lse_pair)
    return highest + jnp.log(summed)


def rescale(own_rows, gradient):
    moved = own_rows.astype(jnp.float32) - step_rate * gradient
    return moved * lax.rsqrt(jnp.mean(moved * moved, axis=1, keepdims=True) + epsilon)


def body(code_rows, centroids):
    rows_total = code_rows.shape[0] * lax.axis_size("item")
    log_rows = jnp.log(jnp.float32(rows_total))
    log_buckets = jnp.log(jnp.float32(BUCKETS))
    potential_col = jnp.zeros((centroids.shape[0],), jnp.float32)
    potential_row = jnp.zeros((code_rows.shape[0],), jnp.float32)
    for iteration in range(ITERS):
        potential_row = -log_rows - reduce_rows(
            scores_of(code_rows, centroids) + potential_col[None, :]
        )
        potential_col = -log_buckets - reduce_cols(
            scores_of(code_rows, centroids) + potential_row[:, None]
        )
    scores = scores_of(code_rows, centroids)
    plan = jnp.exp(scores + potential_row[:, None] + potential_col[None, :] + log_rows)
    masses = jnp.sum(plan, axis=1)
    highest = jnp.max(scores, axis=1)
    totals = jnp.sum(jnp.exp(scores - highest[:, None]), axis=1)
    highest, totals, masses = joined((highest, totals, masses), "bucket", stats_triple)
    delta = (masses[:, None] * jnp.exp(scores - highest[:, None]) / totals[:, None] - plan).astype(
        jnp.bfloat16
    )
    grad_codes = lax.psum(
        score_scale * jnp.dot(delta, centroids, preferred_element_type=jnp.float32), "bucket"
    )
    local_grad = score_scale * lax.dot_general(
        delta, code_rows, (((0,), (0,)), ((), ())), preferred_element_type=jnp.float32
    )
    gradient = lax.psum(local_grad, "item")
    new_centroids = rescale(centroids, gradient)
    return (grad_codes, new_centroids)


def solution(mesh):
    return jax.shard_map(
        body,
        mesh=mesh,
        in_specs=(P("item", None), P("bucket", None)),
        out_specs=(P("item", None), P("bucket", None)),
        check_vma=False,
    )
```

profile of v0, /device:TPU:0, one launch (start us, length us, event | category | flops | bytes accessed | tf_op | source)
XLA Modules:
  0.0 586.0 jit_solution(3918211216739394180)
XLA Ops:
  8.1 14.3 %fusion.2 = (f32[1024]{0:T(1024)S(1)}, f32[1024,8192]{1,0:T(8,128)}) fusion(bf16[1024,64]{0,1:T(8,128)(2,1)S(1)} %copy-done, bf16[8192,64]{0,1:T(8,128)(2,1)} %param.17), kind=kOutput, calls=%fused_computation.49 | convolution fusion | flops 1090518016 | bytes 34738176 | tf_op jit(solution)/shard_map/dot_general | solution.py:22
  22.4 6.2 %all-gather = f32[4096]{0:T(1024)S(1)} all-gather(f32[1024]{0:T(1024)S(1)} %get-tuple-element.326), channel_id=2, replica_groups=mesh['item'=8,'bucket'=4] {'bucket'}, dimensions={0}, use_global_device_ids=true | all-gather | bytes 20480 | tf_op jit(solution)/shard_map/all_gather | solution.py:14
  28.6 13.6 %exponential_reduce_fusion.5 = f32[1024]{0:T(1024)S(1)} fusion(f32[1024,8192]{1,0:T(8,128)} %get-tuple-element.327, f32[1024]{0:T(1024)S(1)} %get-tuple-element.326), kind=kLoop, calls=%fused_computation.29 | loop fusion | flops 16776192 | bytes 33562624 | tf_op jit(solution)/shard_map/reduce_sum | solution.py:80
  47.9 12.5 %add_reduce_fusion.3 = f32[8192]{0:T(1024)S(1)} fusion(f32[1024,8192]{1,0:T(8,128)} %get-tuple-element.327, f32[1024]{0:T(1024)S(1)} %add_subtract_fusion.5), kind=kLoop, calls=%fused_computation.33 | loop fusion | flops 16769024 | bytes 33591296 | tf_op jit(solution)/shard_map/reduce_max | solution.py:52
  60.4 14.0 %exponential_reduce_fusion.4 = f32[8192]{0:T(1024)S(1)} fusion(f32[1024,8192]{1,0:T(8,128)} %get-tuple-element.327, f32[8192]{0:T(1024)S(1)} %add_reduce_fusion.3, f32[1024]{0:T(1024)S(1)} %add_subtract_fusion.5), kind=kLoop, calls=%fused_computation.28 | loop fusion | flops 25157632 | bytes 33624064 | tf_op jit(solution)/shard_map/reduce_sum | solution.py:53
  74.4 31.4 %all-gather.2 = f32[65536]{0:T(1024)S(1)} all-gather(f32[8192]{0:T(1024)S(1)} %add_reduce_fusion.3), channel_id=4, replica_groups=mesh['item'=8,'bucket'=4] {'item'}, dimensions={0}, use_global_device_ids=true | all-gather | bytes 294912 | tf_op jit(solution)/shard_map/all_gather | solution.py:14
  105.8 30.7 %all-gather.3 = f32[65536]{0:T(1024)S(1)} all-gather(f32[8192]{0:T(1024)S(1)} %exponential_reduce_fusion.4), channel_id=5, replica_groups=mesh['item'=8,'bucket'=4] {'item'}, dimensions={0}, use_global_device_ids=true | all-gather | bytes 294912 | tf_op jit(solution)/shard_map/all_gather | solution.py:14
  137.6 12.2 %add_reduce_fusion.2 = f32[1024]{0:T(1024)S(1)} fusion(f32[1024,8192]{1,0:T(8,128)} %get-tuple-element.327, f32[8192]{0:T(1024)S(1)} %add_subtract_fusion.2), kind=kLoop, calls=%fused_computation.32 | loop fusion | flops 16776192 | bytes 33591296 | tf_op jit(solution)/shard_map/reduce_max | solution.py:45
  149.8 14.3 %exponential_reduce_fusion.3 = f32[1024]{0:T(1024)S(1)} fusion(f32[1024,8192]{1,0:T(8,128)} %get-tuple-element.327, f32[1024]{0:T(1024)S(1)} %add_reduce_fusion.2, f32[8192]{0:T(1024)S(1)} %add_subtract_fusion.2), kind=kLoop, calls=%fused_computation.27 | loop fusion | flops 25164800 | bytes 33595392 | tf_op jit(solution)/shard_map/reduce_sum | solution.py:46
  174.7 12.5 %add_reduce_fusion.1 = f32[8192]{0:T(1024)S(1)} fusion(f32[1024,8192]{1,0:T(8,128)} %get-tuple-element.327, f32[1024]{0:T(1024)S(1)} %add_subtract_fusion.4), kind=kLoop, calls=%fused_computation.31 | loop fusion | flops 16769024 | bytes 33591296 | tf_op jit(solution)/shard_map/reduce_max | solution.py:52
  187.2 14.0 %exponential_reduce_fusion.2 = f32[8192]{0:T(1024)S(1)} fusion(f32[1024,8192]{1,0:T(8,128)} %get-tuple-element.327, f32[8192]{0:T(1024)S(1)} %add_reduce_fusion.1, f32[1024]{0:T(1024)S(1)} %add_subtract_fusion.4), kind=kLoop, calls=%fused_computation.26 | loop fusion | flops 25157632 | bytes 33624064 | tf_op jit(solution)/shard_map/reduce_sum | solution.py:53
  201.2 30.9 %all-gather.6 = f32[65536]{0:T(1024)S(1)} all-gather(f32[8192]{0:T(1024)S(1)} %add_reduce_fusion.1), channel_id=8, replica_groups=mesh['item'=8,'bucket'=4] {'item'}, dimensions={0}, use_global_device_ids=true | all-gather | bytes 294912 | tf_op jit(solution)/shard_map/all_gather | solution.py:14
  232.1 30.7 %all-gather.7 = f32[65536]{0:T(1024)S(1)} all-gather(f32[8192]{0:T(1024)S(1)} %exponential_reduce_fusion.2), channel_id=9, replica_groups=mesh['item'=8,'bucket'=4] {'item'}, dimensions={0}, use_global_device_ids=true | all-gather | bytes 294912 | tf_op jit(solution)/shard_map/all_gather | solution.py:14
  263.9 12.2 %add_reduce_fusion = f32[1024]{0:T(1024)S(1)} fusion(f32[1024,8192]{1,0:T(8,128)} %get-tuple-element.327, f32[8192]{0:T(1024)S(1)} %add_subtract_fusion.1), kind=kLoop, calls=%fused_computation.30 | loop fusion | flops 16776192 | bytes 33591296 | tf_op jit(solution)/shard_map/reduce_max | solution.py:45
  276.1 14.3 %exponential_reduce_fusion.1 = f32[1024]{0:T(1024)S(1)} fusion(f32[1024,8192]{1,0:T(8,128)} %get-tuple-element.327, f32[1024]{0:T(1024)S(1)} %add_reduce_fusion, f32[8192]{0:T(1024)S(1)} %add_subtract_fusion.1), kind=kLoop, calls=%fused_computation.25 | loop fusion | flops 25164800 | bytes 33595392 | tf_op jit(solution)/shard_map/reduce_sum | solution.py:46
  301.2 12.5 %add_reduce_fusion.4 = f32[8192]{0:T(1024)S(1)} fusion(f32[1024,8192]{1,0:T(8,128)} %get-tuple-element.327, f32[1024]{0:T(1024)S(1)} %add_subtract_fusion.3), kind=kLoop, calls=%fused_computation.34 | loop fusion | flops 16769024 | bytes 33591296 | tf_op jit(solution)/shard_map/reduce_max | solution.py:52
  313.7 14.0 %exponential_reduce_fusion = f32[8192]{0:T(1024)S(1)} fusion(f32[1024,8192]{1,0:T(8,128)} %get-tuple-element.327, f32[8192]{0:T(1024)S(1)} %add_reduce_fusion.4, f32[1024]{0:T(1024)S(1)} %add_subtract_fusion.3), kind=kLoop, calls=%fused_computation.24 | loop fusion | flops 25157632 | bytes 33624064 | tf_op jit(solution)/shard_map/reduce_sum | solution.py:53
  327.7 30.9 %all-gather.10 = f32[65536]{0:T(1024)S(1)} all-gather(f32[8192]{0:T(1024)S(1)} %add_reduce_fusion.4), channel_id=12, replica_groups=mesh['item'=8,'bucket'=4] {'item'}, dimensions={0}, use_global_device_ids=true | all-gather | bytes 294912 | tf_op jit(solution)/shard_map/all_gather | solution.py:14
  358.6 30.7 %all-gather.11 = f32[65536]{0:T(1024)S(1)} all-gather(f32[8192]{0:T(1024)S(1)} %exponential_reduce_fusion), channel_id=13, replica_groups=mesh['item'=8,'bucket'=4] {'item'}, dimensions={0}, use_global_device_ids=true | all-gather | bytes 294912 | tf_op jit(solution)/shard_map/all_gather | solution.py:14
  390.4 14.8 %fusion = f32[1024]{0:T(1024)S(1)} fusion(f32[1024,8192]{1,0:T(8,128)} %get-tuple-element.327, f32[8192]{0:T(1024)S(1)} %add_subtract_fusion, f32[1024]{0:T(1024)S(1)} %add_subtract_fusion.3), kind=kLoop, calls=%fused_computation.35 | loop fusion | flops 33553408 | bytes 33595392 | tf_op jit(solution)/shard_map/reduce_sum | solution.py:78
  410.7 18.8 %subtract_convert_fusion = bf16[1024,8192]{1,0:T(8,128)(2,1)S(1)} fusion(f32[1024,8192]{1,0:T(8,128)} %get-tuple-element.327, f32[1024]{0:T(1024)S(1)} %get-tuple-element.223, f32[1024]{0:T(1024)S(1)} %get-tuple-element.222, f32[1024]{0:T(1024)S(1)} %get-tuple-element.221, f32[8192]{0:T(1024)S(1)} %add_subtract_fusion, f32[1024]{0:T(1024)S(1)} %add_subtract_fusion.3), kind=kLoop, calls=%fused_computation.22 | loop fusion | flops 67108864 | bytes 50380800 | tf_op jit(solution)/shard_map/convert_element_type | solution.py:82
  439.8 11.7 %convolution_multiply_fusion.1 = f32[1024,64]{0,1:T(8,128)} fusion(bf16[1024,8192]{1,0:T(8,128)(2,1)} %copy-done.1, bf16[8192,64]{0,1:T(8,128)(2,1)S(1)} %copy-done.2), kind=kOutput, calls=%fused_computation.41 | convolution fusion | flops 1073807360 | bytes 18087936 | tf_op jit(solution)/shard_map/dot_general | solution.py:86
  451.5 91.4 %all-reduce.5.cloned.1.call-done = f32[8192,64]{0,1:T(8,128)} async-done(((f32[8192,64]{0,1:T(8,128)}), f32[8192,64]{0,1:T(8,128)}) %all-reduce.5.cloned.1.call-update) | async-done | bytes 2097168 | tf_op jit(solution)/shard_map/psum | solution.py:91
  548.2 29.2 %all-reduce.3.cloned.1.call-done = f32[1024,64]{0,1:T(8,128)} async-done(((f32[1024,64]{0,1:T(8,128)}), f32[1024,64]{0,1:T(8,128)}) %all-reduce.3.cloned.1.call-update) | async-done | bytes 262160 | tf_op jit(solution)/shard_map/psum | solution.py:85
  (147 shorter events, 56.4 us)
Async XLA Ops:
  7.2 0.9 copy-start
  7.2 535.8 %all-reduce.5.cloned.1.call-start = ((), (), s32[]{:S(2)}) async-start(), calls=%async_computation.1 | async-start | bytes 4194304 | tf_op jit(solution)/shard_map/psum | solution.py:91
  410.6 29.2 %copy-start.2 = (bf16[8192,64]{0,1:T(8,128)(2,1)S(1)}, bf16[8192,64]{0,1:T(8,128)(2,1)}, u32[]{:S(2)}) copy-start(bf16[8192,64]{0,1:T(8,128)(2,1)} %param.17) | copy-start | bytes 3145732
  429.5 5.7 copy-start.1
  439.5 137.9 %all-reduce.3.cloned.1.call-start = ((), (), s32[]{:S(2)}) async-start(), calls=%async_computation | async-start | bytes 524288 | tf_op jit(solution)/shard_map/psum | solution.py:85
Sparse Core Ops, SparseCore 0:
  439.7 103.2 all-reduce.4
  545.9 31.5 all-reduce.2
where the time goes:
time: 588 us; the launch traced here: 586 us
  blocking collectives  223 us (38%)
  other arithmetic  186 us (32%)
  waiting for transfers between devices  121 us (21%)
  matrix products  30.3 us (5%)
  between operations  14.4 us (2%)
  local copies, waits for them, and re-layouts  10.4 us (2%)
    all_gather x13, blocking collectives, joined(): pieces = jax.tree.map(lambda part: lax.all_gather(part, axis), value)  223 us
    psum x1, waiting for transfers between devices, body(): gradient = lax.psum(local_grad, 'item')  91.4 us
    reduce_sum x3, other arithmetic, reduce_cols(): summed = jnp.sum(jnp.exp(values - highest[None, :]), axis=0)  41.9 us
    reduce_max x3, other arithmetic, reduce_cols(): highest = jnp.max(values, axis=0)  37.4 us
    psum x1, waiting for transfers between devices, body(): lax.psum(score_scale * jnp.dot(delta, centroids, preferred_element_type=j...  29.2 us
    reduce_sum x2, other arithmetic, reduce_rows(): summed = jnp.sum(jnp.exp(values - highest[:, None]), axis=1)  28.6 us
    reduce_max x2, other arithmetic, reduce_rows(): highest = jnp.max(values, axis=1)  24.3 us
    convert_element_type x1, other arithmetic, body(): (masses[:, None] * jnp.exp(scores - highest[:, None]) / totals[:, None] -...  18.8 us
  transfers between devices with their start and end apart: 2, of which 2 were waited for; matrix products, arithmetic and copies ran while one was open for 3% of the time, Pallas kernels for 0%

commit v1 on v0

--- a/solution.py
+++ b/solution.py
@@ -1,3 +1,4 @@
+import functools
 import jax
 import jax.numpy as jnp
 from jax import lax
@@ -8,6 +9,19 @@
 score_scale = 20.0
 step_rate = 0.2
 epsilon = 1e-06
+
+
+def edit_loops_for(mine_x, axis_name):
+    nd = lax.psum(1, axis_name)
+    r1 = lambda newest: [(dev_i, dev_i ^ newest) for dev_i in range(nd)]
+    found_now = mine_x
+    for kk in range(nd.bit_length() - 1):
+        x_now = lax.ppermute(found_now, axis_name, r1(1 << kk))
+        found_now = found_now + x_now
+    return found_now
+
+
+choose_counts = functools.partial(edit_loops_for, axis_name="item")
 
 
 def joined(value, axis, join):
@@ -88,7 +102,7 @@
     local_grad = score_scale * lax.dot_general(
         delta, code_rows, (((0,), (0,)), ((), ())), preferred_element_type=jnp.float32
     )
-    gradient = lax.psum(local_grad, "item")
+    gradient = choose_counts(local_grad)
     new_centroids = rescale(centroids, gradient)
     return (grad_codes, new_centroids)
 

time: 588 us -> 636 us (1.082)
  waiting for transfers between devices: 121 us -> 177 us
  matrix products: 30.3 us -> 23.2 us
    ppermute x0 -> x3, waiting for transfers between devices: none -> 177 us  [edit_loops_for(): x_now = lax.ppermute(found_now, axis_name, r1(1 << kk))]
    psum x1 -> x0, waiting for transfers between devices: 91.4 us -> none  [body(): gradient = lax.psum(local_grad, 'item')]
    psum x1, waiting for transfers between devices: 29.2 us -> 0.01 us  [body(): lax.psum(score_scale * jnp.dot(delta, centroids, preferred_element_type=j...]
  transfers between devices with their start and end apart: 2 -> 4, of which waited for: 2 -> 3; matrix products, arithmetic and copies ran while one was open for 3% -> 2% of each run, Pallas kernels for 0% -> 0%
where the time goes in v1:
time: 636 us; the launch traced here: 634 us
  blocking collectives  223 us (35%)
  other arithmetic  187 us (29%)
  waiting for transfers between devices  177 us (28%)
  matrix products  23.2 us (4%)
  between operations  14.4 us (2%)
    all_gather x13, blocking collectives, joined(): pieces = jax.tree.map(lambda part: lax.all_gather(part, axis), value)  223 us
    ppermute x3, waiting for transfers between devices, edit_loops_for(): x_now = lax.ppermute(found_now, axis_name, r1(1 << kk))  177 us
    reduce_sum x3, other arithmetic, reduce_cols(): summed = jnp.sum(jnp.exp(values - highest[None, :]), axis=0)  41.9 us
    reduce_max x3, other arithmetic, reduce_cols(): highest = jnp.max(values, axis=0)  37.4 us
    reduce_sum x2, other arithmetic, reduce_rows(): summed = jnp.sum(jnp.exp(values - highest[:, None]), axis=1)  28.6 us
    reduce_max x2, other arithmetic, reduce_rows(): highest = jnp.max(values, axis=1)  24.3 us
    convert_element_type x1, other arithmetic, body(): (masses[:, None] * jnp.exp(scores - highest[:, None]) / totals[:, None] -...  18.8 us
    reduce_sum x1, other arithmetic, body(): masses = jnp.sum(plan, axis=1)  14.8 us
  transfers between devices with their start and end apart: 4, of which 3 were waited for; matrix products, arithmetic and copies ran while one was open for 2% of the time, Pallas kernels for 0%

profile of v1, /device:TPU:0, one launch (start us, length us, event | category | flops | bytes accessed | tf_op | source)
XLA Modules:
  0.0 634.4 jit_solution(14887621685138847062)
XLA Ops:
  8.1 14.3 %fusion.1 = (f32[1024]{0:T(1024)S(1)}, f32[1024,8192]{1,0:T(8,128)}) fusion(bf16[1024,64]{0,1:T(8,128)(2,1)S(1)} %copy-done, bf16[8192,64]{0,1:T(8,128)(2,1)} %param.17), kind=kOutput, calls=%fused_computation.49 | convolution fusion | flops 1090518016 | bytes 34738176 | tf_op jit(solution)/shard_map/dot_general | solution.py:36
  22.4 6.2 all-gather
  28.6 13.6 %exponential_reduce_fusion.5 = f32[1024]{0:T(1024)S(1)} fusion(f32[1024,8192]{1,0:T(8,128)} %get-tuple-element.327, f32[1024]{0:T(1024)S(1)} %get-tuple-element.326), kind=kLoop, calls=%fused_computation.29 | loop fusion | flops 16776192 | bytes 33562624 | tf_op jit(solution)/shard_map/reduce_sum | solution.py:94
  47.9 12.5 %add_reduce_fusion.3 = f32[8192]{0:T(1024)S(1)} fusion(f32[1024,8192]{1,0:T(8,128)} %get-tuple-element.327, f32[1024]{0:T(1024)S(1)} %add_subtract_fusion.5), kind=kLoop, calls=%fused_computation.33 | loop fusion | flops 16769024 | bytes 33591296 | tf_op jit(solution)/shard_map/reduce_max | solution.py:66
  60.4 14.0 %exponential_reduce_fusion.4 = f32[8192]{0:T(1024)S(1)} fusion(f32[1024,8192]{1,0:T(8,128)} %get-tuple-element.327, f32[8192]{0:T(1024)S(1)} %add_reduce_fusion.3, f32[1024]{0:T(1024)S(1)} %add_subtract_fusion.5), kind=kLoop, calls=%fused_computation.28 | loop fusion | flops 25157632 | bytes 33624064 | tf_op jit(solution)/shard_map/reduce_sum | solution.py:67
  74.4 31.4 %all-gather.2 = f32[65536]{0:T(1024)S(1)} all-gather(f32[8192]{0:T(1024)S(1)} %add_reduce_fusion.3), channel_id=4, replica_groups=mesh['item'=8,'bucket'=4] {'item'}, dimensions={0}, use_global_device_ids=true | all-gather | bytes 294912 | tf_op jit(solution)/shard_map/all_gather | solution.py:28
  105.8 30.7 %all-gather.3 = f32[65536]{0:T(1024)S(1)} all-gather(f32[8192]{0:T(1024)S(1)} %exponential_reduce_fusion.4), channel_id=5, replica_groups=mesh['item'=8,'bucket'=4] {'item'}, dimensions={0}, use_global_device_ids=true | all-gather | bytes 294912 | tf_op jit(solution)/shard_map/all_gather | solution.py:28
  137.6 12.2 %add_reduce_fusion.2 = f32[1024]{0:T(1024)S(1)} fusion(f32[1024,8192]{1,0:T(8,128)} %get-tuple-element.327, f32[8192]{0:T(1024)S(1)} %add_subtract_fusion.2), kind=kLoop, calls=%fused_computation.32 | loop fusion | flops 16776192 | bytes 33591296 | tf_op jit(solution)/shard_map/reduce_max | solution.py:59
  149.8 14.3 %exponential_reduce_fusion.3 = f32[1024]{0:T(1024)S(1)} fusion(f32[1024,8192]{1,0:T(8,128)} %get-tuple-element.327, f32[1024]{0:T(1024)S(1)} %add_reduce_fusion.2, f32[8192]{0:T(1024)S(1)} %add_subtract_fusion.2), kind=kLoop, calls=%fused_computation.27 | loop fusion | flops 25164800 | bytes 33595392 | tf_op jit(solution)/shard_map/reduce_sum | solution.py:60
  174.7 12.5 %add_reduce_fusion.1 = f32[8192]{0:T(1024)S(1)} fusion(f32[1024,8192]{1,0:T(8,128)} %get-tuple-element.327, f32[1024]{0:T(1024)S(1)} %add_subtract_fusion.4), kind=kLoop, calls=%fused_computation.31 | loop fusion | flops 16769024 | bytes 33591296 | tf_op jit(solution)/shard_map/reduce_max | solution.py:66
  187.2 14.0 %exponential_reduce_fusion.2 = f32[8192]{0:T(1024)S(1)} fusion(f32[1024,8192]{1,0:T(8,128)} %get-tuple-element.327, f32[8192]{0:T(1024)S(1)} %add_reduce_fusion.1, f32[1024]{0:T(1024)S(1)} %add_subtract_fusion.4), kind=kLoop, calls=%fused_computation.26 | loop fusion | flops 25157632 | bytes 33624064 | tf_op jit(solution)/shard_map/reduce_sum | solution.py:67
  201.2 30.9 %all-gather.6 = f32[65536]{0:T(1024)S(1)} all-gather(f32[8192]{0:T(1024)S(1)} %add_reduce_fusion.1), channel_id=8, replica_groups=mesh['item'=8,'bucket'=4] {'item'}, dimensions={0}, use_global_device_ids=true | all-gather | bytes 294912 | tf_op jit(solution)/shard_map/all_gather | solution.py:28
  232.1 30.7 %all-gather.7 = f32[65536]{0:T(1024)S(1)} all-gather(f32[8192]{0:T(1024)S(1)} %exponential_reduce_fusion.2), channel_id=9, replica_groups=mesh['item'=8,'bucket'=4] {'item'}, dimensions={0}, use_global_device_ids=true | all-gather | bytes 294912 | tf_op jit(solution)/shard_map/all_gather | solution.py:28
  263.9 12.2 %add_reduce_fusion = f32[1024]{0:T(1024)S(1)} fusion(f32[1024,8192]{1,0:T(8,128)} %get-tuple-element.327, f32[8192]{0:T(1024)S(1)} %add_subtract_fusion.1), kind=kLoop, calls=%fused_computation.30 | loop fusion | flops 16776192 | bytes 33591296 | tf_op jit(solution)/shard_map/reduce_max | solution.py:59
  276.1 14.3 %exponential_reduce_fusion.1 = f32[1024]{0:T(1024)S(1)} fusion(f32[1024,8192]{1,0:T(8,128)} %get-tuple-element.327, f32[1024]{0:T(1024)S(1)} %add_reduce_fusion, f32[8192]{0:T(1024)S(1)} %add_subtract_fusion.1), kind=kLoop, calls=%fused_computation.25 | loop fusion | flops 25164800 | bytes 33595392 | tf_op jit(solution)/shard_map/reduce_sum | solution.py:60
  301.2 12.5 %add_reduce_fusion.4 = f32[8192]{0:T(1024)S(1)} fusion(f32[1024,8192]{1,0:T(8,128)} %get-tuple-element.327, f32[1024]{0:T(1024)S(1)} %add_subtract_fusion.3), kind=kLoop, calls=%fused_computation.34 | loop fusion | flops 16769024 | bytes 33591296 | tf_op jit(solution)/shard_map/reduce_max | solution.py:66
  313.7 14.0 %exponential_reduce_fusion = f32[8192]{0:T(1024)S(1)} fusion(f32[1024,8192]{1,0:T(8,128)} %get-tuple-element.327, f32[8192]{0:T(1024)S(1)} %add_reduce_fusion.4, f32[1024]{0:T(1024)S(1)} %add_subtract_fusion.3), kind=kLoop, calls=%fused_computation.24 | loop fusion | flops 25157632 | bytes 33624064 | tf_op jit(solution)/shard_map/reduce_sum | solution.py:67
  327.7 30.9 %all-gather.10 = f32[65536]{0:T(1024)S(1)} all-gather(f32[8192]{0:T(1024)S(1)} %add_reduce_fusion.4), channel_id=12, replica_groups=mesh['item'=8,'bucket'=4] {'item'}, dimensions={0}, use_global_device_ids=true | all-gather | bytes 294912 | tf_op jit(solution)/shard_map/all_gather | solution.py:28
  358.6 30.7 %all-gather.11 = f32[65536]{0:T(1024)S(1)} all-gather(f32[8192]{0:T(1024)S(1)} %exponential_reduce_fusion), channel_id=13, replica_groups=mesh['item'=8,'bucket'=4] {'item'}, dimensions={0}, use_global_device_ids=true | all-gather | bytes 294912 | tf_op jit(solution)/shard_map/all_gather | solution.py:28
  390.4 14.8 %fusion = f32[1024]{0:T(1024)S(1)} fusion(f32[1024,8192]{1,0:T(8,128)} %get-tuple-element.327, f32[8192]{0:T(1024)S(1)} %add_subtract_fusion, f32[1024]{0:T(1024)S(1)} %add_subtract_fusion.3), kind=kLoop, calls=%fused_computation.35 | loop fusion | flops 33553408 | bytes 33595392 | tf_op jit(solution)/shard_map/reduce_sum | solution.py:92
  410.7 18.8 %subtract_convert_fusion = bf16[1024,8192]{1,0:T(8,128)(2,1)S(1)} fusion(f32[1024,8192]{1,0:T(8,128)} %get-tuple-element.327, f32[1024]{0:T(1024)S(1)} %get-tuple-element.223, f32[1024]{0:T(1024)S(1)} %get-tuple-element.222, f32[1024]{0:T(1024)S(1)} %get-tuple-element.221, f32[8192]{0:T(1024)S(1)} %add_subtract_fusion, f32[1024]{0:T(1024)S(1)} %add_subtract_fusion.3), kind=kLoop, calls=%fused_computation.22 | loop fusion | flops 67108864 | bytes 50380800 | tf_op jit(solution)/shard_map/convert_element_type | solution.py:96
  434.1 46.4 %collective-permute-done = f32[8192,64]{0,1:T(8,128)S(1)} collective-permute-done((f32[8192,64]{0,1:T(8,128)S(1)}, f32[8192,64]{0,1:T(8,128)S(1)}, u32[]{:S(2)}, u32[]{:S(2)}) %collective-permute-start) | collective-permute-done | bytes 2097184 | tf_op jit(solution)/shard_map/ppermute | solution.py:19
  480.7 47.0 %collective-permute-done.1 = f32[8192,64]{0,1:T(8,128)S(1)} collective-permute-done((f32[8192,64]{0,1:T(8,128)S(1)}, f32[8192,64]{0,1:T(8,128)S(1)}, u32[]{:S(2)}, u32[]{:S(2)}) %collective-permute-start.1) | collective-permute-done | bytes 2097184 | tf_op jit(solution)/shard_map/ppermute | solution.py:19
  536.1 84.1 %collective-permute-done.2 = f32[8192,64]{0,1:T(8,128)} collective-permute-done((f32[8192,64]{0,1:T(8,128)S(1)}, f32[8192,64]{0,1:T(8,128)}, u32[]{:S(2)}, u32[]{:S(2)}) %collective-permute-start.2) | collective-permute-done | bytes 2097184 | tf_op jit(solution)/shard_map/ppermute | solution.py:19
  (150 shorter events, 59.7 us)
Async XLA Ops:
  7.2 0.9 copy-start
  7.2 618.7 %all-reduce.2.cloned.1.call-start = ((), (), s32[]{:S(2)}) async-start(), calls=%async_computation | async-start | bytes 524288 | tf_op jit(solution)/shard_map/psum | solution.py:99
  410.6 119.5 %copy-start.1 = (bf16[8192,64]{0,1:T(8,128)(2,1)S(1)}, bf16[8192,64]{0,1:T(8,128)(2,1)}, u32[]{:S(2)}) copy-start(bf16[8192,64]{0,1:T(8,128)(2,1)} %param.17) | copy-start | bytes 3145732
  432.5 47.9 %collective-permute-start = (f32[8192,64]{0,1:T(8,128)S(1)}, f32[8192,64]{0,1:T(8,128)S(1)}, u32[]{:S(2)}, u32[]{:S(2)}) collective-permute-start(f32[8192,64]{0,1:T(8,128)S(1)} %convolution_multiply_fusion), channel_id=1, source_target_pairs={{0,4},{4,0},{8,12},{12,8},{16,20},{20,16},{24,28},{28,24},{1,5},{5... | collective-permute-start | bytes 6291464 | tf_op jit(solution)/shard_map/ppermute | solution.py:19
  480.7 47.1 %collective-permute-start.1 = (f32[8192,64]{0,1:T(8,128)S(1)}, f32[8192,64]{0,1:T(8,128)S(1)}, u32[]{:S(2)}, u32[]{:S(2)}) collective-permute-start(f32[8192,64]{0,1:T(8,128)S(1)} %add.163), channel_id=1, source_target_pairs={{0,8},{4,12},{8,0},{12,4},{16,24},{20,28},{24,16},{28,20},{1,9},{5... | collective-permute-start | bytes 6291464 | tf_op jit(solution)/shard_map/ppermute | solution.py:19
  528.0 92.2 %collective-permute-start.2 = (f32[8192,64]{0,1:T(8,128)S(1)}, f32[8192,64]{0,1:T(8,128)}, u32[]{:S(2)}, u32[]{:S(2)}) collective-permute-start(f32[8192,64]{0,1:T(8,128)S(1)} %add.164), channel_id=1, source_target_pairs={{0,16},{4,20},{8,24},{12,28},{16,0},{20,4},{24,8},{28,12},{1,17},{... | collective-permute-start | bytes 6291464 | tf_op jit(solution)/shard_map/ppermute | solution.py:19
Sparse Core Ops, SparseCore 0:
  536.2 31.6 all-reduce.1
